TPU v7x, 32 devices: a whole 2x2x4 slice. The times are simulated.
32 devices in a mesh: groups: 2 (over x), mp: 8 (over z, y), row: 2 (over core).
Axes of the slice: x: 2, y: 2, z: 4, core: 2. Of those that a mesh axis runs over, the one named last changes fastest.
Arguments:
- stream: bfloat16 [2, 256, 4096], P(None, ('groups', 'row'), 'mp'), parts along dimension 1, may hold values from -12 to 12
- projected: bfloat16 [2, 256, 2, 8192], P(None, ('groups', 'row'), None, 'mp'), parts along dimension 1, may hold values from -6 to 6
- conv_state: bfloat16 [256, 3, 8192], P(('groups', 'row'), None, 'mp'), parts along dimension 0, may hold values from -6 to 6
- scan_state: float32 [256, 16, 8192], P(('groups', 'row'), None, 'mp'), parts along dimension 0, may hold values from -6 to 6
- conv_weight: float32 [4, 8192], P(None, 'mp'), may hold values from -3 to 3
- conv_bias: float32 [8192], P('mp'), may hold values from -3 to 3
- state_proj: bfloat16 [8192, 288], P('mp'), may hold values from -0.0625 to 0.0625
- step_proj: bfloat16 [256, 8192], P(None, 'mp'), may hold values from -0.375 to 0.375
- step_bias: float32 [8192], P('mp'), may hold values from -3 to 0.5
- decay_log: float32 [16, 8192], P(None, 'mp'), may hold values from -4 to 2
- skip_gain: float32 [8192], P('mp'), may hold values from 0.25 to 1.75
- out_weight: bfloat16 [8192, 4096], P('mp'), may hold values from -0.09375 to 0.09375
- norm_gain: float32 [4096], replicated, may hold values from 0.25 to 1.75
- router: bfloat16 [16, 4096], replicated, may hold values from -0.09375 to 0.09375
- expert_gate: bfloat16 [2, 4096, 12288], P('row', None, 'mp'), may hold values from -0.09375 to 0.09375
- expert_up: bfloat16 [2, 4096, 12288], P('row', None, 'mp'), may hold values from -0.09375 to 0.09375
- expert_down: bfloat16 [2, 12288, 4096], P('row', 'mp'), may hold values from -0.078125 to 0.078125
- expert_ids: int32 [2, 256, 2], P(None, ('groups', 'row')), parts along dimension 1, may hold values from 0 to 15, as said below
Outputs:
- mixed_out: bfloat16 [2, 256, 4096], P(None, ('groups', 'row'), 'mp'), parts along dimension 1
- new_state: float32 [256, 16, 8192], P(('groups', 'row'), None, 'mp'), parts along dimension 0
There are 2 independent parts, one for each index of `groups`. A program takes and returns all parts, laid end to end along the dimension named above; an argument that names none is the same for every part. Nothing has to cross between parts.
Inputs may be any that keep to these rules, and one draw needn't show every extreme that they name: `expert_ids`: A row's two ids differ. In each step, at most 16 of the rows of one device (aligned blocks of 64 rows) choose expert 0, and at most 16 choose expert 1; in every draw some step has exactly 16 such rows for both experts in every block.
All inputs are finite; a program needn't handle non-finite values.
Results may differ from a plain program's by a relative error of at most 0.006.
Values may be sent and summed in bfloat16 or wider, within the bound.
A program may use at most 128 MiB of HBM per device.

v0:
```python
import jax
import jax.numpy as jnp
from jax import lax
from jax.sharding import PartitionSpec as P

CAP = 16


def expert_apply(tokens_in, gate_weight, up_weight, down_weight):
    gate_part = jnp.dot(tokens_in, gate_weight, preferred_element_type=jnp.float32)
    up_part = jnp.dot(tokens_in, up_weight, preferred_element_type=jnp.float32)
    hidden = (jax.nn.silu(gate_part) * up_part).astype(jnp.bfloat16)
    return jnp.dot(hidden, down_weight, preferred_element_type=jnp.float32)


def on_device(
    stream,
    projected,
    conv_state,
    scan_state,
    conv_weight,
    conv_bias,
    state_proj,
    step_proj,
    step_bias,
    decay_log,
    skip_gain,
    out_weight,
    norm_gain,
    router,
    expert_gate,
    expert_up,
    expert_down,
    expert_ids,
):
    step_count, row_count, width_local = stream.shape
    inner_local = projected.shape[3]
    kernel_size = conv_weight.shape[0]
    rank_size = step_proj.shape[0]
    state_size = decay_log.shape[0]
    full_width = out_weight.shape[1]
    flat_rows = step_count * row_count
    inputs = projected[:, :, 0, :]
    gate_side = projected[:, :, 1, :]
    history = jnp.concatenate(
        [conv_state.astype(jnp.float32), jnp.transpose(inputs, (1, 0, 2)).astype(jnp.float32)],
        axis=1,
    )
    conv_list = []
    for step_no in range(step_count):
        window = history[:, step_no : step_no + kernel_size, :]
        conv_list.append(
            jax.nn.silu(jnp.sum(window * conv_weight[None], axis=1) + conv_bias).astype(
                jnp.bfloat16
            )
        )
    convolved = jnp.stack(conv_list)
    local_proj = jnp.dot(
        convolved.reshape(flat_rows, inner_local), state_proj, preferred_element_type=jnp.float32
    )
    projections = lax.psum(local_proj, "mp").reshape(step_count, row_count, -1)
    low_rank = projections[..., :rank_size].astype(jnp.bfloat16)
    input_gain = projections[..., rank_size : rank_size + state_size]
    output_gain = projections[..., rank_size + state_size :]
    timestep = jax.nn.softplus(
        jnp.dot(
            low_rank.reshape(flat_rows, rank_size), step_proj, preferred_element_type=jnp.float32
        ).reshape(step_count, row_count, inner_local)
        + step_bias
    )
    decay_rates = jnp.exp(decay_log)
    carried = scan_state
    outputs = []
    for step_no in range(step_count):
        current = convolved[step_no].astype(jnp.float32)
        delta_now = timestep[step_no]
        decay_now = jnp.exp(-delta_now[:, None, :] * decay_rates[None])
        carried = (
            decay_now * carried
            + (delta_now * current)[:, None, :] * input_gain[step_no][:, :, None]
        )
        readout = jnp.sum(output_gain[step_no][:, :, None] * carried, axis=1) + skip_gain * current
        outputs.append(
            (readout * jax.nn.silu(gate_side[step_no].astype(jnp.float32))).astype(jnp.bfloat16)
        )
    scanned = jnp.stack(outputs).reshape(flat_rows, inner_local)
    partial_value = jnp.dot(scanned, out_weight, preferred_element_type=jnp.float32)
    offset = lax.axis_index("mp") * width_local
    own_part = stream.reshape(flat_rows, width_local).astype(jnp.float32)
    placed = lax.dynamic_update_slice_in_dim(
        partial_value,
        lax.dynamic_slice_in_dim(partial_value, offset, width_local, 1) + own_part,
        offset,
        1,
    )
    after_full = lax.psum(placed, "mp").astype(jnp.bfloat16)
    after_own = lax.dynamic_slice_in_dim(after_full, offset, width_local, 1)
    widened = after_full.astype(jnp.float32)
    normed = (
        widened * lax.rsqrt(jnp.mean(widened * widened, axis=-1, keepdims=True) + 1e-05) * norm_gain
    ).astype(jnp.bfloat16)
    logits = lax.dot_general(
        normed, router, (((1,), (1,)), ((), ())), preferred_element_type=jnp.float32
    )
    picked = expert_ids.reshape(flat_rows, -1)
    expert_total = router.shape[0]
    onehot = picked[:, :, None] == jnp.arange(expert_total)[None, None, :]
    chosen = jnp.sum(jnp.where(onehot, logits[:, None, :], 0.0), axis=2)
    weights = jnp.exp(chosen)
    shares = weights / jnp.sum(weights, axis=1, keepdims=True)
    in_flight = lax.axis_size("row")
    weight_rows = jnp.stack(
        [jnp.sum(jnp.where(picked == expert, shares, 0.0), axis=1) for expert in range(in_flight)],
        axis=1,
    )
    gate_weight = expert_gate[0]
    up_weight = expert_up[0]
    down_weight = expert_down[0]
    routed = jnp.any(picked[:, None, :] == jnp.arange(in_flight)[None, :, None], axis=2)
    position = (
        jnp.cumsum(routed.reshape(step_count, row_count, in_flight).astype(jnp.int32), axis=1) - 1
    ).reshape(flat_rows, in_flight)
    slot_total = step_count * CAP
    slot_index = jnp.arange(slot_total)
    row_step = jnp.arange(flat_rows) // row_count
    matching = (
        jnp.transpose(routed)[:, None, :]
        & (row_step[None, None, :] == (slot_index // CAP)[None, :, None])
        & (jnp.transpose(position)[:, None, :] == (slot_index % CAP)[None, :, None])
    )
    select_half = matching.astype(jnp.bfloat16)
    select_full = matching.astype(jnp.float32)
    outgoing = jnp.einsum(
        "esm,mx->esx", select_half, normed, preferred_element_type=jnp.float32
    ).astype(jnp.bfloat16)
    slot_share = jnp.einsum("esm,me->es", select_full, weight_rows, precision=lax.Precision.HIGHEST)
    arrived = lax.all_to_all(outgoing, "row", split_axis=0, concat_axis=0, tiled=True)
    count_here = arrived.shape[1]
    produced = expert_apply(
        arrived.reshape(-1, full_width), gate_weight, up_weight, down_weight
    ).reshape(in_flight, count_here, full_width)
    returned = lax.all_to_all(
        produced.astype(jnp.bfloat16), "row", split_axis=0, concat_axis=0, tiled=True
    ).astype(produced.dtype)
    combined = jnp.einsum(
        "esm,esx->mx",
        select_full,
        returned * slot_share[:, :, None],
        precision=lax.Precision.HIGHEST,
    )
    combined = lax.psum_scatter(combined, "mp", scatter_dimension=1, tiled=True)
    mixed_out = (
        (after_own.astype(jnp.float32) + combined)
        .astype(jnp.bfloat16)
        .reshape(step_count, row_count, width_local)
    )
    return (mixed_out, carried)


def solution(mesh):
    return jax.shard_map(
        on_device,
        mesh=mesh,
        in_specs=(
            P(None, ("groups", "row"), "mp"),
            P(None, ("groups", "row"), None, "mp"),
            P(("groups", "row"), None, "mp"),
            P(("groups", "row"), None, "mp"),
            P(None, "mp"),
            P("mp"),
            P("mp", None),
            P(None, "mp"),
            P("mp"),
            P(None, "mp"),
            P("mp"),
            P("mp", None),
            P(),
            P(),
            P("row", None, "mp"),
            P("row", None, "mp"),
            P("row", "mp", None),
            P(None, ("groups", "row"), None),
        ),
        out_specs=(P(None, ("groups", "row"), "mp"), P(("groups", "row"), None, "mp")),
        check_vma=False,
    )
```

profile of v0, /device:TPU:0, one launch (start us, length us, event | category | flops | bytes accessed | tf_op | source)
XLA Modules:
  0.0 296.4 jit_solution(5089809884289274848)
XLA Ops:
  7.2 1.2 copy.64
  8.5 1.1 maximum_convert_fusion
  9.6 0.9 fusion.19
  10.8 1.1 fusion.59
  12.0 0.6 fusion.58
  13.1 72.3 %all-reduce.3.cloned.1.call-done = f32[2,64,288]{2,1,0:T(8,128)} async-done(((f32[2,64,288]{2,1,0:T(8,128)}), f32[2,64,288]{2,1,0:T(8,128)}) %all-reduce.3.cloned.1.call-update) | async-done | bytes 147472 | tf_op jit(solution)/shard_map/psum | solution.py:61
  85.4 1.5 compare_select_fusion
  87.1 0.9 slice_bitcast_fusion.5
  88.1 7.0 %multiply_reduce_fusion = (f32[64,1024]{1,0:T(8,128)S(1)}, f32[64,16,1024]{2,1,0:T(8,128)}, f32[64,1024]{1,0:T(8,128)S(1)}) fusion(f32[64,16]{1,0:T(8,128)S(1)} %get-tuple-element.17, f32[64,16]{1,0:T(8,128)S(1)} %get-tuple-element.16, f32[64,1024]{1,0:T(8,128)S(1)} %get-tuple-element.10, f32[64,16]{1,0:T(8,128)S(1)} %get-tuple-element.18, ...), kind=kLoop, calls=%fused_computation.9 | loop fusion | flops 12451840 | bytes 10043392 | tf_op jit(solution)/shard_map/reduce_sum | solution.py:82
  95.1 0.2 fusion.40
  95.4 1.3 fusion.60
  96.7 92.4 %all-reduce.4 = bf16[128,4096]{1,0:T(8,128)(2,1)} all-reduce(f32[128,4096]{1,0:T(8,128)S(1)} %fusion.38), channel_id=1, replica_groups=mesh['groups'=2,'mp'=8,'row'=2] {'mp'}, use_global_device_ids=true, to_apply=%region_5.6 | all-reduce | flops 524288 | bytes 3145728 | tf_op jit(solution)/shard_map/psum | solution.py:96
  189.1 1.5 fusion.15
  190.7 1.7 fusion.27
  192.8 1.9 convolution_convert_fusion
  194.9 4.2 %all_to_all.10 = bf16[2,32,4096]{2,1,0:T(8,128)(2,1)S(1)} all-to-all(bf16[2,32,4096]{2,1,0:T(8,128)(2,1)S(1)} %convolution_convert_fusion), channel_id=1, replica_groups=mesh['groups'=2,'mp'=8,'row'=2] {'row'}, dimensions={0} | all-to-all | bytes 1048576 | tf_op jit(solution)/shard_map/all_to_all | solution.py:137
  199.1 7.0 %fusion.4 = f32[64,1536]{1,0:T(8,128)S(1)} fusion(bf16[64,4096]{1,0:T(8,128)(2,1)S(1)} %bitcast.119, bf16[1,4096,1536]{2,1,0:T(8,128)(2,1)} %param.32), kind=kOutput, calls=%fused_computation.4 | convolution fusion | flops 805306368 | bytes 13500416 | tf_op jit(solution)/shard_map/dot_general | solution.py:10
  206.1 2.3 fusion.12
  208.5 1.4 slice-done.7
  209.9 2.3 fusion.6
  212.2 4.2 %all_to_all.11 = bf16[2,32,4096]{2,1,0:T(8,128)(2,1)S(1)} all-to-all(bf16[2,32,4096]{2,1,0:T(8,128)(2,1)S(1)} %fusion.6), channel_id=1, replica_groups=mesh['groups'=2,'mp'=8,'row'=2] {'row'}, dimensions={0} | all-to-all | bytes 1048576 | tf_op jit(solution)/shard_map/all_to_all | solution.py:142
  216.4 2.4 convolution_bitcast_fusion
  218.8 69.1 %reduce-scatter.2.cloned.1.call-done = f32[128,512]{1,0:T(8,128)} async-done(((f32[128,4096]{1,0:T(8,128)}), f32[128,512]{1,0:T(8,128)}) %reduce-scatter.2.cloned.1.call-update) | async-done | bytes 262160 | tf_op jit(solution)/shard_map/reduce_scatter | solution.py:151
  287.9 1.7 add_convert_fusion
  (73 shorter events, 1.9 us)
Async XLA Ops:
  7.2 3.6 %copy-start = (bf16[1024,288]{0,1:T(8,128)(2,1)S(1)}, bf16[1024,288]{0,1:T(8,128)(2,1)}, u32[]{:S(2)}) copy-start(bf16[1024,288]{0,1:T(8,128)(2,1)} %param.24) | copy-start | bytes 1769476
  7.2 4.8 %copy-start.2 = (bf16[2,64,2,1024]{3,2,1,0:T(2,128)(2,1)S(1)}, bf16[2,64,2,1024]{3,2,1,0:T(2,128)(2,1)}, u32[]{:S(2)}) copy-start(bf16[2,64,2,1024]{3,2,1,0:T(2,128)(2,1)} %param.19) | copy-start | bytes 1572868
  7.2 3.4 %copy-start.5 = (f32[1024]{0:T(1024)S(1)}, f32[1024]{0:T(1024)}, u32[]{:S(2)}) copy-start(f32[1024]{0:T(1024)} %param.23) | copy-start | bytes 12292
  7.2 78.2 %all-reduce.3.cloned.1.call-start = ((), (), s32[]{:S(2)}) async-start(), calls=%async_computation.3 | async-start | bytes 393216 | tf_op jit(solution)/shard_map/psum | solution.py:61
  8.5 4.1 %copy-start.6 = (s32[2,64,2]{1,2,0:T(2,128)S(1)}, s32[2,64,2]{1,2,0:T(2,128)}, u32[]{:S(2)}) copy-start(s32[2,64,2]{1,2,0:T(2,128)} %param.35) | copy-start | bytes 3076
  8.5 4.5 %copy-start.4 = (f32[16,1024]{1,0:T(8,128)S(1)}, f32[16,1024]{1,0:T(8,128)}, u32[]{:S(2)}) copy-start(f32[16,1024]{1,0:T(8,128)} %param.27) | copy-start | bytes 196612
  8.5 77.0 %copy-start.8 = (bf16[256,1024]{1,0:T(8,128)(2,1)S(1)}, bf16[256,1024]{1,0:T(8,128)(2,1)}, u32[]{:S(2)}) copy-start(bf16[256,1024]{1,0:T(8,128)(2,1)} %param.25) | copy-start | bytes 1572868
  8.5 76.9 %copy-start.11 = (f32[1024]{0:T(1024)S(1)}, f32[1024]{0:T(1024)}, u32[]{:S(2)}) copy-start(f32[1024]{0:T(1024)} %param.26) | copy-start | bytes 12292
  11.9 276.0 %reduce-scatter.2.cloned.1.call-start = ((), (), s32[]{:S(2)}) async-start(), calls=%async_computation.4 | async-start | bytes 2359296 | tf_op jit(solution)/shard_map/reduce_scatter | solution.py:151
  85.4 9.9 %slice-start.3 = ((s8[8388608]{0:T(1024)(128)(4,1)}), s8[4194304]{0:T(1024)(128)(4,1)S(1)}, s32[]{:S(2)}) async-start(s8[8388608]{0:T(1024)(128)(4,1)} %bitcast.115), calls=%async_computation.8 | async-start | bytes 8388608
  88.1 7.0 %copy-start.7 = (f32[1024]{0:T(1024)S(1)}, f32[1024]{0:T(1024)}, u32[]{:S(2)}) copy-start(f32[1024]{0:T(1024)} %param.28) | copy-start | bytes 12292
  88.1 7.3 %slice-start.4 = ((s8[8388608]{0:T(1024)(128)(4,1)}), s8[4194304]{0:T(1024)(128)(4,1)S(1)}, s32[]{:S(2)}) async-start(s8[8388608]{0:T(1024)(128)(4,1)} %bitcast.115), calls=%async_computation.9 | async-start | bytes 8388608
  95.3 1.3 copy-start.3
  96.7 94.0 %copy-start.9 = (bf16[16,4096]{1,0:T(8,128)(2,1)S(1)}, bf16[16,4096]{1,0:T(8,128)(2,1)}, u32[]{:S(2)}) copy-start(bf16[16,4096]{1,0:T(8,128)(2,1)} %param.31) | copy-start | bytes 393220
  96.7 94.0 %copy-start.10 = (f32[4096]{0:T(1024)S(1)}, f32[4096]{0:T(1024)}, u32[]{:S(2)}) copy-start(f32[4096]{0:T(1024)} %param.30) | copy-start | bytes 49156
  192.8 13.3 %slice-start = ((s8[12582912]{0:T(1024)(128)(4,1)}), s8[4194304]{0:T(1024)(128)(4,1)S(1)}, s32[]{:S(2)}) async-start(s8[12582912]{0:T(1024)(128)(4,1)} %bitcast.113), calls=%async_computation.5 | async-start | bytes 8388608
  199.0 7.0 %slice-start.1 = ((s8[12582912]{0:T(1024)(128)(4,1)}), s8[4194304]{0:T(1024)(128)(4,1)S(1)}, s32[]{:S(2)}) async-start(s8[12582912]{0:T(1024)(128)(4,1)} %bitcast.113), calls=%async_computation.6 | async-start | bytes 8388608
  199.1 7.0 %slice-start.2 = ((s8[12582912]{0:T(1024)(128)(4,1)}), s8[4194304]{0:T(1024)(128)(4,1)S(1)}, s32[]{:S(2)}) async-start(s8[12582912]{0:T(1024)(128)(4,1)} %bitcast.113), calls=%async_computation.7 | async-start | bytes 8388608
  199.1 9.3 %slice-start.5 = ((s8[12582912]{0:T(1024)(128)(4,1)}), s8[4194304]{0:T(1024)(128)(4,1)S(1)}, s32[]{:S(2)}) async-start(s8[12582912]{0:T(1024)(128)(4,1)} %bitcast.117), calls=%async_computation.10 | async-start | bytes 8388608
  199.1 9.4 %slice-start.6 = ((s8[12582912]{0:T(1024)(128)(4,1)}), s8[4194304]{0:T(1024)(128)(4,1)S(1)}, s32[]{:S(2)}) async-start(s8[12582912]{0:T(1024)(128)(4,1)} %bitcast.117), calls=%async_computation.11 | async-start | bytes 8388608
  206.1 3.8 %slice-start.7 = ((s8[12582912]{0:T(1024)(128)(4,1)}), s8[4194304]{0:T(1024)(128)(4,1)S(1)}, s32[]{:S(2)}) async-start(s8[12582912]{0:T(1024)(128)(4,1)} %bitcast.117), calls=%async_computation.12 | async-start | bytes 8388608
  209.9 79.7 %copy-start.1 = (bf16[1024,288]{0,1:T(8,128)(2,1)S(1)}, bf16[1024,288]{0,1:T(8,128)(2,1)}, u32[]{:S(2)}) copy-start(bf16[1024,288]{0,1:T(8,128)(2,1)} %param.24) | copy-start | bytes 1769476
Sparse Core Ops, SparseCore 0:
  12.0 73.3 all-reduce.2
  218.9 68.9 reduce-scatter.1
where the time goes:
time: 297 us; the launch traced here: 296 us
  waiting for transfers between devices  141 us (47%)
  blocking collectives  101 us (34%)
  matrix products  21.6 us (7%)
  between operations  14.4 us (5%)
  other arithmetic  13.2 us (4%)
  local copies, waits for them, and re-layouts  4.98 us (2%)
    psum x1, blocking collectives, on_device(): after_full = lax.psum(placed, 'mp').astype(jnp.bfloat16)  92.4 us
    psum x1, waiting for transfers between devices, on_device(): projections = lax.psum(local_proj, 'mp').reshape(step_count, row_count, -1)  72.3 us
    reduce_scatter x1, waiting for transfers between devices, on_device(): combined = lax.psum_scatter(combined, 'mp', scatter_dimension=1, tiled=True)  69.1 us
    reduce_sum x1, other arithmetic, on_device(): jnp.sum(output_gain[step_no][:, :, None] * carried, axis=1)  6.97 us
    dot_general x1, matrix products, expert_apply(): jnp.dot(tokens_in, gate_weight, preferred_element_type=jnp.float32)  6.97 us
  transfers between devices with their start and end apart: 2, of which 2 were waited for; matrix products, arithmetic and copies ran while one was open for 0% of the time, Pallas kernels for 0%

commit v1 on v0

--- a/solution.py
+++ b/solution.py
@@ -2,6 +2,7 @@
 import jax.numpy as jnp
 from jax import lax
 from jax.sharding import PartitionSpec as P
+from jax.lax import all_gather
 
 CAP = 16
 
@@ -58,7 +59,7 @@
     local_proj = jnp.dot(
         convolved.reshape(flat_rows, inner_local), state_proj, preferred_element_type=jnp.float32
     )
-    projections = lax.psum(local_proj, "mp").reshape(step_count, row_count, -1)
+    projections = jnp.sum(all_gather(local_proj, "mp"), axis=0).reshape(step_count, row_count, -1)
     low_rank = projections[..., :rank_size].astype(jnp.bfloat16)
     input_gain = projections[..., rank_size : rank_size + state_size]
     output_gain = projections[..., rank_size + state_size :]

time: 297 us -> 265 us (0.89)
  waiting for transfers between devices: 141 us -> 111 us
    psum x1 -> x0, waiting for transfers between devices: 72.3 us -> none  [on_device(): projections = lax.psum(local_proj, 'mp').reshape(step_count, row_count, -1)]
    all_gather x0 -> x1, waiting for transfers between devices: none -> 42 us  [on_device(): all_gather(local_proj, 'mp')]
where the time goes in v1:
time: 265 us
  waiting for transfers between devices  111 us (42%)
  blocking collectives  99.8 us (38%)
  matrix products  20.5 us (8%)
  between operations  14.4 us (5%)
  other arithmetic  13.7 us (5%)
  local copies, waits for them, and re-layouts  5.78 us (2%)
    psum x1, blocking collectives, on_device(): after_full = lax.psum(placed, 'mp').astype(jnp.bfloat16)  91.5 us
    reduce_scatter x1, waiting for transfers between devices, on_device(): combined = lax.psum_scatter(combined, 'mp', scatter_dimension=1, tiled=True)  68.6 us
    all_gather x1, waiting for transfers between devices, on_device(): all_gather(local_proj, 'mp')  42 us
    reduce_sum x1, other arithmetic, on_device(): jnp.sum(output_gain[step_no][:, :, None] * carried, axis=1)  7.22 us
    dot_general x1, matrix products, expert_apply(): jnp.dot(tokens_in, gate_weight, preferred_element_type=jnp.float32)  6.97 us
  transfers between devices with their start and end apart: 2, of which 2 were waited for; matrix products, arithmetic and copies ran while one was open for 0% of the time, Pallas kernels for 0%

profile of v1, /device:TPU:0, one launch (start us, length us, event | category | flops | bytes accessed | tf_op | source)
XLA Modules:
  0.0 264.9 jit_solution(13403900074671189723)
XLA Ops:
  7.3 1.2 copy.74
  8.5 1.1 maximum_convert_fusion
  9.6 0.9 fusion.19
  10.8 1.0 fusion.59
  12.4 0.6 fusion.58
  12.9 42.0 %all-gather.3.cloned.1.call-done = f32[1024,288]{0,1:T(8,128)} async-done(((f32[128,288]{0,1:T(8,128)}), f32[1024,288]{0,1:T(8,128)}) %all-gather.3.cloned.1.call-update) | async-done | bytes 1179664 | tf_op jit(solution)/shard_map/all_gather | solution.py:62
  55.0 1.5 copy.64
  56.5 0.3 bitcast_reduce_fusion
  57.0 0.5 compare_select_fusion
  57.7 7.2 %multiply_reduce_fusion = (f32[64,1024]{1,0:T(8,128)S(1)}, f32[64,16,1024]{2,1,0:T(8,128)}, f32[64,1024]{1,0:T(8,128)S(1)}) fusion(f32[64,16]{1,0:T(8,128)S(1)} %get-tuple-element.17, f32[64,16]{1,0:T(8,128)S(1)} %get-tuple-element.16, f32[64,1024]{1,0:T(8,128)S(1)} %get-tuple-element.10, f32[64,16]{1,0:T(8,128)S(1)} %get-tuple-element.18, ...), kind=kLoop, calls=%fused_computation.9 | loop fusion | flops 12451840 | bytes 10043392 | tf_op jit(solution)/shard_map/reduce_sum | solution.py:83
  65.2 1.3 fusion.60
  66.6 91.5 %all-reduce.1 = bf16[128,4096]{1,0:T(8,128)(2,1)} all-reduce(f32[128,4096]{1,0:T(8,128)S(1)} %fusion.38), channel_id=1, replica_groups=mesh['groups'=2,'mp'=8,'row'=2] {'mp'}, use_global_device_ids=true, to_apply=%region_5.6 | all-reduce | flops 524288 | bytes 3145728 | tf_op jit(solution)/shard_map/psum | solution.py:97
  158.1 1.5 fusion.15
  159.6 1.7 fusion.27
  161.7 1.9 convolution_convert_fusion
  163.8 4.2 %all_to_all.10 = bf16[2,32,4096]{2,1,0:T(8,128)(2,1)S(1)} all-to-all(bf16[2,32,4096]{2,1,0:T(8,128)(2,1)S(1)} %convolution_convert_fusion), channel_id=1, replica_groups=mesh['groups'=2,'mp'=8,'row'=2] {'row'}, dimensions={0} | all-to-all | bytes 1048576 | tf_op jit(solution)/shard_map/all_to_all | solution.py:138
  168.0 7.0 %fusion.4 = f32[64,1536]{1,0:T(8,128)S(1)} fusion(bf16[64,4096]{1,0:T(8,128)(2,1)S(1)} %bitcast.124, bf16[1,4096,1536]{2,1,0:T(8,128)(2,1)} %param.32), kind=kOutput, calls=%fused_computation.4 | convolution fusion | flops 805306368 | bytes 13500416 | tf_op jit(solution)/shard_map/dot_general | solution.py:11
  175.1 2.3 fusion.12
  177.4 1.4 slice-done.7
  178.9 2.3 fusion.6
  181.2 4.2 %all_to_all.11 = bf16[2,32,4096]{2,1,0:T(8,128)(2,1)S(1)} all-to-all(bf16[2,32,4096]{2,1,0:T(8,128)(2,1)S(1)} %fusion.6), channel_id=1, replica_groups=mesh['groups'=2,'mp'=8,'row'=2] {'row'}, dimensions={0} | all-to-all | bytes 1048576 | tf_op jit(solution)/shard_map/all_to_all | solution.py:143
  185.3 2.4 convolution_bitcast_fusion
  187.8 68.6 %reduce-scatter.2.cloned.1.call-done = f32[128,512]{1,0:T(8,128)} async-done(((f32[128,4096]{1,0:T(8,128)}), f32[128,512]{1,0:T(8,128)}) %reduce-scatter.2.cloned.1.call-update) | async-done | bytes 262160 | tf_op jit(solution)/shard_map/reduce_scatter | solution.py:152
  256.4 1.7 add_convert_fusion
  (76 shorter events, 2.4 us)
Async XLA Ops:
  7.2 3.6 %copy-start = (bf16[1024,288]{0,1:T(8,128)(2,1)S(1)}, bf16[1024,288]{0,1:T(8,128)(2,1)}, u32[]{:S(2)}) copy-start(bf16[1024,288]{0,1:T(8,128)(2,1)} %param.24) | copy-start | bytes 1769476
  7.2 3.4 %copy-start.5 = (f32[1024]{0:T(1024)S(1)}, f32[1024]{0:T(1024)}, u32[]{:S(2)}) copy-start(f32[1024]{0:T(1024)} %param.23) | copy-start | bytes 12292
  7.2 4.6 %copy-start.6 = (s32[2,64,2]{1,2,0:T(2,128)S(1)}, s32[2,64,2]{1,2,0:T(2,128)}, u32[]{:S(2)}) copy-start(s32[2,64,2]{1,2,0:T(2,128)} %param.35) | copy-start | bytes 3076
  7.2 5.0 %copy-start.4 = (f32[16,1024]{1,0:T(8,128)S(1)}, f32[16,1024]{1,0:T(8,128)}, u32[]{:S(2)}) copy-start(f32[16,1024]{1,0:T(8,128)} %param.27) | copy-start | bytes 196612
  7.2 47.8 %all-gather.3.cloned.1.call-start = ((), (), s32[]{:S(2)}) async-start(), calls=%async_computation.4 | async-start | bytes 1327104 | tf_op jit(solution)/shard_map/all_gather | solution.py:62
  7.3 5.1 %copy-start.2 = (bf16[2,64,2,1024]{3,2,1,0:T(2,128)(2,1)S(1)}, bf16[2,64,2,1024]{3,2,1,0:T(2,128)(2,1)}, u32[]{:S(2)}) copy-start(bf16[2,64,2,1024]{3,2,1,0:T(2,128)(2,1)} %param.19) | copy-start | bytes 1572868
  10.5 46.5 %copy-start.8 = (bf16[256,1024]{1,0:T(8,128)(2,1)S(1)}, bf16[256,1024]{1,0:T(8,128)(2,1)}, u32[]{:S(2)}) copy-start(bf16[256,1024]{1,0:T(8,128)(2,1)} %param.25) | copy-start | bytes 1572868
  10.5 46.5 %copy-start.11 = (f32[1024]{0:T(1024)S(1)}, f32[1024]{0:T(1024)}, u32[]{:S(2)}) copy-start(f32[1024]{0:T(1024)} %param.26) | copy-start | bytes 12292
  11.8 244.7 %reduce-scatter.2.cloned.1.call-start = ((), (), s32[]{:S(2)}) async-start(), calls=%async_computation.3 | async-start | bytes 2359296 | tf_op jit(solution)/shard_map/reduce_scatter | solution.py:152
  57.0 8.2 %slice-start.3 = ((s8[8388608]{0:T(1024)(128)(4,1)}), s8[4194304]{0:T(1024)(128)(4,1)S(1)}, s32[]{:S(2)}) async-start(s8[8388608]{0:T(1024)(128)(4,1)} %bitcast.120), calls=%async_computation.8 | async-start | bytes 8388608
  57.7 7.2 %copy-start.7 = (f32[1024]{0:T(1024)S(1)}, f32[1024]{0:T(1024)}, u32[]{:S(2)}) copy-start(f32[1024]{0:T(1024)} %param.28) | copy-start | bytes 12292
  57.7 7.5 %slice-start.4 = ((s8[8388608]{0:T(1024)(128)(4,1)}), s8[4194304]{0:T(1024)(128)(4,1)S(1)}, s32[]{:S(2)}) async-start(s8[8388608]{0:T(1024)(128)(4,1)} %bitcast.120), calls=%async_computation.9 | async-start | bytes 8388608
  65.2 1.3 copy-start.3
  66.5 93.1 %copy-start.9 = (bf16[16,4096]{1,0:T(8,128)(2,1)S(1)}, bf16[16,4096]{1,0:T(8,128)(2,1)}, u32[]{:S(2)}) copy-start(bf16[16,4096]{1,0:T(8,128)(2,1)} %param.31) | copy-start | bytes 393220
  66.5 93.1 %copy-start.10 = (f32[4096]{0:T(1024)S(1)}, f32[4096]{0:T(1024)}, u32[]{:S(2)}) copy-start(f32[4096]{0:T(1024)} %param.30) | copy-start | bytes 49156
  161.7 13.3 %slice-start = ((s8[12582912]{0:T(1024)(128)(4,1)}), s8[4194304]{0:T(1024)(128)(4,1)S(1)}, s32[]{:S(2)}) async-start(s8[12582912]{0:T(1024)(128)(4,1)} %bitcast.118), calls=%async_computation.5 | async-start | bytes 8388608
  168.0 7.0 %slice-start.1 = ((s8[12582912]{0:T(1024)(128)(4,1)}), s8[4194304]{0:T(1024)(128)(4,1)S(1)}, s32[]{:S(2)}) async-start(s8[12582912]{0:T(1024)(128)(4,1)} %bitcast.118), calls=%async_computation.6 | async-start | bytes 8388608
  168.0 7.0 %slice-start.2 = ((s8[12582912]{0:T(1024)(128)(4,1)}), s8[4194304]{0:T(1024)(128)(4,1)S(1)}, s32[]{:S(2)}) async-start(s8[12582912]{0:T(1024)(128)(4,1)} %bitcast.118), calls=%async_computation.7 | async-start | bytes 8388608
  168.0 9.3 %slice-start.5 = ((s8[12582912]{0:T(1024)(128)(4,1)}), s8[4194304]{0:T(1024)(128)(4,1)S(1)}, s32[]{:S(2)}) async-start(s8[12582912]{0:T(1024)(128)(4,1)} %bitcast.122), calls=%async_computation.10 | async-start | bytes 8388608
  168.0 9.4 %slice-start.6 = ((s8[12582912]{0:T(1024)(128)(4,1)}), s8[4194304]{0:T(1024)(128)(4,1)S(1)}, s32[]{:S(2)}) async-start(s8[12582912]{0:T(1024)(128)(4,1)} %bitcast.122), calls=%async_computation.11 | async-start | bytes 8388608
  175.1 3.8 %slice-start.7 = ((s8[12582912]{0:T(1024)(128)(4,1)}), s8[4194304]{0:T(1024)(128)(4,1)S(1)}, s32[]{:S(2)}) async-start(s8[12582912]{0:T(1024)(128)(4,1)} %bitcast.122), calls=%async_computation.12 | async-start | bytes 8388608
  178.9 79.2 %copy-start.1 = (bf16[1024,288]{0,1:T(8,128)(2,1)S(1)}, bf16[1024,288]{0,1:T(8,128)(2,1)}, u32[]{:S(2)}) copy-start(bf16[1024,288]{0,1:T(8,128)(2,1)} %param.24) | copy-start | bytes 1769476
Sparse Core Ops, SparseCore 0:
  11.9 43.0 all-gather.2
  187.9 68.4 reduce-scatter.1
